TPU v7x, 256 devices: a whole 4x4x8 slice. The times are simulated.
256 devices in a mesh: seq: 32 (over z, x), head: 8 (over y, core).
Axes of the slice: x: 4, y: 4, z: 8, core: 2. Of those that a mesh axis runs over, the one named last changes fastest.
Arguments:
- corpus: bfloat16 [128, 128, 4096], P('seq'), may hold values from -8 to 8
- enc_qkv: bfloat16 [4096, 16, 3, 128], P(None, 'head'), may hold values from -0.1015625 to 0.1015625
- enc_out: bfloat16 [16, 128, 4096], P('head'), may hold values from -0.375 to 0.375
- cca_kv: bfloat16 [4096, 16, 2, 128], P('seq', 'head'), may hold values from -0.09375 to 0.09375
- gain_in: float32 [4096], replicated, may hold values from 0.5 to 2
- gain_out: float32 [4096], replicated, may hold values from 0.5 to 2
- queries: bfloat16 [16384, 16, 128], P('seq', 'head'), may hold values from -100 to 100
- nbr_ids: int32 [256, 2], P('seq'), may hold values from 0 to 127, as said below
Outputs:
- cca_out: bfloat16 [16384, 16, 128], P('seq', 'head')
Inputs may be any that keep to these rules, and one draw needn't show every extreme that they name: `nbr_ids`: entry [u, n] is the corpus row of group u's n-th neighbour; row r is held by index r // 4 of seq. The neighbours of one group differ. Among the requests of the 8 groups of one index of seq no owner is named more than 2 times, and in every draw some owner is named exactly 2 times by every index of seq.
All inputs are finite; a program needn't handle non-finite values.
Results may differ from a plain program's by a relative error of at most 0.03.
Values may be sent and summed in bfloat16 or wider, within the bound.
No kernel may reach another device: no remote copies, remote signals or barrier semaphores. Data moves between devices by JAX's collectives and lax.ppermute only.
A program may use at most 128 MiB of HBM per device.

v0:
```python
import jax
import jax.numpy as jnp
from jax import lax
from jax.sharding import PartitionSpec as P

GROUP = 64
NBRS = 2
CAP = 2
EPS = 1e-06


def passed_along(value, axis, steps):
    count = lax.axis_size(axis)
    first, last = (max(0, -steps), min(count, count - steps))
    return lax.ppermute(value, axis, [(source, source + steps) for source in range(first, last)])


def rms_scale(values, gain):
    mean_square = jnp.mean(values * values, axis=-1, keepdims=True)
    return values * lax.rsqrt(mean_square + EPS) * gain


def attend(query_blocks, key_blocks, value_blocks):
    scale = query_blocks.shape[-1] ** (-0.5)
    scores = (
        jnp.einsum("bqhs,bkhs->bhqk", query_blocks, key_blocks, preferred_element_type=jnp.float32)
        * scale
    )
    probs = jax.nn.softmax(scores, axis=-1).astype(jnp.bfloat16)
    return jnp.einsum("bhqk,bkhs->bqhs", probs, value_blocks, preferred_element_type=jnp.float32)


def on_device(corpus, enc_qkv, enc_out, cca_kv, gain_in, gain_out, queries, nbr_ids):
    corp_rows, row_tokens, model_width = corpus.shape
    heads_here = enc_qkv.shape[1]
    head_size = enc_qkv.shape[3]
    row_total = corp_rows * row_tokens
    corpus_flat = corpus.reshape(row_total, model_width)
    normed_in = rms_scale(corpus_flat.astype(jnp.float32), gain_in).astype(jnp.bfloat16)
    projected = jnp.dot(
        normed_in,
        enc_qkv.reshape(model_width, heads_here * 3 * head_size),
        preferred_element_type=jnp.float32,
    )
    projected = projected.astype(jnp.bfloat16).reshape(
        corp_rows, row_tokens, heads_here, 3, head_size
    )
    attended = attend(projected[:, :, :, 0], projected[:, :, :, 1], projected[:, :, :, 2]).astype(
        jnp.bfloat16
    )
    attended = attended.reshape(row_total, heads_here * head_size)
    out_weight = enc_out.reshape(heads_here * head_size, model_width)
    partial_terms = jnp.dot(attended, out_weight, preferred_element_type=jnp.float32)
    enc_sum = lax.psum(partial_terms, "head")
    normed = rms_scale(corpus_flat.astype(jnp.float32) + enc_sum, gain_out).astype(jnp.bfloat16)
    memory_cols = heads_here * 2 * head_size
    shard_piece = lax.all_gather(cca_kv, "seq", axis=0, tiled=True)
    memory = jnp.dot(
        normed,
        shard_piece.reshape(shard_piece.shape[0], memory_cols),
        preferred_element_type=jnp.float32,
    )
    memory = memory.astype(jnp.bfloat16).reshape(corp_rows, row_tokens, heads_here, 2, head_size)
    request_ids = nbr_ids.reshape(-1)
    demand = request_ids.shape[0]
    owners = request_ids // corp_rows
    local_row = request_ids % corp_rows
    request_order = jnp.arange(demand)
    earlier = request_order[None, :] < request_order[:, None]
    same_owner = owners[:, None] == owners[None, :]
    slot_rank = jnp.sum(jnp.logical_and(same_owner, earlier), axis=1)
    slot_index = owners * CAP + slot_rank
    devices = lax.axis_size("seq")
    positions = jnp.arange(devices * CAP)
    matched = positions[:, None] == slot_index[None, :]
    wanted = jnp.sum(jnp.where(matched, local_row[None, :], 0), axis=1).reshape(devices, CAP)
    picked = jnp.take(
        memory, lax.all_to_all(wanted, "seq", split_axis=0, concat_axis=0, tiled=True), axis=0
    )
    fetched = lax.all_to_all(picked, "seq", split_axis=0, concat_axis=0, tiled=True)
    fetched = fetched.reshape(devices * CAP, row_tokens, heads_here, 2, head_size)
    group_memory = jnp.take(fetched, slot_index, axis=0)
    groups_here = nbr_ids.shape[0]
    group_memory = group_memory.reshape(groups_here, NBRS * row_tokens, heads_here, 2, head_size)
    token_count = queries.shape[0]
    lead = GROUP - 1
    before = passed_along(group_memory[groups_here - 1 :], "seq", 1)
    window_memory = jnp.concatenate([before, group_memory], axis=0)
    padded_queries = jnp.concatenate(
        [
            jnp.zeros((1, heads_here, head_size), jnp.bfloat16),
            queries,
            jnp.zeros((lead, heads_here, head_size), jnp.bfloat16),
        ],
        axis=0,
    ).reshape(groups_here + 1, GROUP, heads_here, head_size)
    extended = attend(padded_queries, window_memory[:, :, :, 0], window_memory[:, :, :, 1])
    extended = extended.reshape((groups_here + 1) * GROUP, heads_here, head_size)
    result = extended[1 : 1 + token_count].astype(jnp.bfloat16)
    return result


def solution(mesh):
    placed = (
        P("seq", None, None),
        P(None, "head", None, None),
        P("head", None, None),
        P("seq", "head", None, None),
        P(),
        P(),
        P("seq", "head", None),
        P("seq", None),
    )
    return jax.shard_map(
        on_device, mesh=mesh, in_specs=placed, out_specs=P("seq", "head", None), check_vma=False
    )
```

profile of v0, /device:TPU:104, one launch (start us, length us, event | category | flops | bytes accessed | tf_op | source)
XLA Modules:
  0.0 442.4 jit_solution(8818635364731222058)
XLA Ops:
  7.4 16.4 %copy.108 = bf16[4096,2,3,128]{0,3,2,1:T(8,128)(2,1)} copy(bf16[4096,2,3,128]{3,1,2,0:T(2,128)(2,1)} %param.9) | data formatting | bytes 12582912 | tf_op args[1]
  23.8 3.2 multiply_reduce_fusion.1
  27.2 1.7 multiply_convert_fusion.1
  28.9 1.1 copy-done.3
  30.0 3.5 convolution_convert_fusion
  33.5 1.2 copy.109
  34.6 1.7 reshape.286
  36.4 1.0 fusion.50
  37.4 0.2 copy.129
  37.6 0.2 copy.130
  37.8 0.3 convolution_multiply_fusion.1
  38.1 0.4 fusion.51
  38.5 1.3 fusion.19
  39.9 4.5 %fusion.22 = f32[512,4096]{1,0:T(8,128)} fusion(bf16[256,4096]{1,0:T(8,128)(2,1)S(1)} %bitcast.79, bf16[64,8,2,128]{3,2,1,0:T(2,128)(2,1)S(1)} %bitcast.85), kind=kOutput, calls=%fused_computation.38 | convolution fusion | flops 1073741824 | bytes 10747904 | tf_op jit(solution)/shard_map/dot_general | solution.py:53
  44.5 0.5 all-gather.2.cloned.1.call-update
  45.7 16.9 %all_to_all.20 = s32[32,1,2]{2,1,0:T(1,128)S(1)} all-to-all(s32[32,1,2]{2,1,0:T(1,128)S(1)} %bitcast.88), channel_id=1, replica_groups=mesh['seq'=32,'head'=8] {'seq'}, dimensions={0} | all-to-all | bytes 512 | tf_op jit(solution)/shard_map/all_to_all | solution.py:78
  63.0 90.3 %all-reduce.2.cloned.1.call-done = f32[512,4096]{1,0:T(8,128)} async-done(((f32[512,4096]{1,0:T(8,128)}), f32[512,4096]{1,0:T(8,128)}) %all-reduce.2.cloned.1.call-update) | async-done | bytes 8388624 | tf_op jit(solution)/shard_map/psum | solution.py:54
  153.3 8.9 %multiply_reduce_fusion = (f32[512]{0:T(512)S(1)}, f32[512,4096]{1,0:T(8,128)}) fusion(f32[512,4096]{1,0:T(8,128)} %all-reduce.2.cloned.1.call-done, bf16[4,128,4096]{2,1,0:T(8,128)(2,1)} %param.8), kind=kLoop, calls=%fused_computation.7 | loop fusion | flops 8388096 | bytes 20973568 | tf_op jit(solution)/shard_map/reduce_sum | solution.py:19
  162.2 7.2 %reshape.289 = bf16[4096,512]{1,0:T(8,128)(2,1)} reshape(bf16[4096,2,2,128]{3,2,1,0:T(2,128)(2,1)} %all-gather.2.cloned.1.call-done) | data formatting | bytes 8388608 | tf_op jit(solution)/shard_map/reshape | solution.py:60
  169.4 6.9 %fusion.7 = bf16[512,512]{1,0:T(8,128)(2,1)S(1)} fusion(bf16[4096,512]{1,0:T(8,128)(2,1)} %reshape.289, f32[512,4096]{1,0:T(8,128)} %get-tuple-element.8, f32[4096]{0:T(1024)S(1)} %copy-done.7, f32[512]{0:T(512)S(1)} %add_rsqrt_fusion), kind=kOutput, calls=%fused_computation.20 | convolution fusion | flops 2154037248 | bytes 13125632 | tf_op jit(solution)/shard_map/dot_general | solution.py:58
  176.5 18.3 %gather_fusion = bf16[64,128,2,2,128]{4,3,2,1,0:T(2,128)(2,1)} fusion(bf16[4,128,2,2,128]{4,3,2,1,0:T(2,128)(2,1)S(1)} %reshape.290, s32[1024]{0:T(1024)S(1)} %pad_clamp_fusion.1), kind=kCustom, calls=%fused_computation | custom fusion | bytes 16777472 | tf_op jit(solution)/shard_map/jit(_take)/gather | solution.py:77
  194.8 7.7 %copy_select_fusion = bf16[32,2,128,2,2,128]{5,2,4,3,1,0:T(8,128)(2,1)} fusion(bf16[32,2,128,2,2,128]{5,4,3,2,1,0:T(2,128)(2,1)} %bitcast.80, pred[32,2]{1,0:T(8,128)(4,1)S(1)} %copy.107), kind=kLoop, calls=%fused_computation.5 | loop fusion | flops 4194304 | bytes 16777280 | tf_op jit(solution)/shard_map/jit(_take)/select_n | solution.py:77
  202.6 10.0 %all-to-all-start.1 = ((bf16[32,2,128,2,2,128]{5,2,4,3,1,0:T(8,128)(2,1)}), bf16[32,2,128,2,2,128]{5,2,4,3,1,0:T(8,128)(2,1)}, u32[]{:S(2)}, u32[]{:S(2)}) async-start(bf16[32,2,128,2,2,128]{5,2,4,3,1,0:T(8,128)(2,1)} %copy_select_fusion), calls=%async_computation.1 | async-start | bytes 16777216 | tf_op jit(solution)/shard_map/all_to_all | solution.py:80
  213.2 0.2 maximum_maximum_fusion
  213.4 198.6 %all-to-all-done.1 = bf16[32,2,128,2,2,128]{5,2,4,3,1,0:T(8,128)(2,1)} async-done(((bf16[32,2,128,2,2,128]{5,2,4,3,1,0:T(8,128)(2,1)}), bf16[32,2,128,2,2,128]{5,2,4,3,1,0:T(8,128)(2,1)}, u32[]{:S(2)}, u32[]{:S(2)}) %all-to-all-start.1) | async-done | bytes 8388640 | tf_op jit(solution)/shard_map/all_to_all | solution.py:80
  412.0 4.3 gather_fusion.1
  416.6 1.9 collective-permute-start
  418.5 1.6 copy_select_fusion.1
  420.1 8.8 %collective-permute-done = bf16[1,256,2,2,128]{4,1,2,0,3:T(8,128)(2,1)S(1)} collective-permute-done((bf16[1,256,2,2,128]{4,1,2,0,3:T(8,128)(2,1)S(1)}, bf16[1,256,2,2,128]{4,1,2,0,3:T(8,128)(2,1)S(1)}, u32[]{:S(2)}, u32[]{:S(2)}) %collective-permute-start) | collective-permute-done | bytes 262176 | tf_op jit(solution)/shard_map/ppermute | solution.py:15
  428.8 3.1 fusion.56
  431.9 2.0 fusion.16
  434.0 1.0 copy.126
  (54 shorter events, 2.5 us)
Async XLA Ops:
  7.4 32.6 %copy-start = (bf16[2,128,4096]{2,1,0:T(8,128)(2,1)S(1)}, bf16[2,128,4096]{2,1,0:T(8,128)(2,1)}, u32[]{:S(2)}) copy-start(bf16[2,128,4096]{2,1,0:T(8,128)(2,1)} %param.10) | copy-start | bytes 6291460
  7.4 145.9 %all-reduce.2.cloned.1.call-start = ((), (), s32[]{:S(2)}) async-start(), calls=%async_computation.2 | async-start | bytes 16777216 | tf_op jit(solution)/shard_map/psum | solution.py:54
  7.4 19.6 %copy-start.5 = (f32[4096]{0:T(1024)S(1)}, f32[4096]{0:T(1024)}, u32[]{:S(2)}) copy-start(f32[4096]{0:T(1024)} %param.12) | copy-start | bytes 49156
  23.8 3.4 copy-start.2
  27.2 2.8 copy-start.3
  44.4 0.7 copy-start.6
  44.4 117.7 %all-gather.2.cloned.1.call-start = ((), (), s32[]{:S(2)}) async-start(), calls=%async_computation.3 | async-start | bytes 4325376 | tf_op jit(solution)/shard_map/all_gather | solution.py:57
  162.1 7.3 %copy-start.7 = (f32[4096]{0:T(1024)S(1)}, f32[4096]{0:T(1024)}, u32[]{:S(2)}) copy-start(f32[4096]{0:T(1024)} %param.13) | copy-start | bytes 49156
  202.6 10.3 %copy-start.4 = (bf16[512,2,128]{2,1,0:T(2,128)(2,1)S(1)}, bf16[512,2,128]{2,1,0:T(2,128)(2,1)}, u32[]{:S(2)}) copy-start(bf16[512,2,128]{2,1,0:T(2,128)(2,1)} %param.14) | copy-start | bytes 786436
  202.6 209.4 %all-to-all-start.1 = ((bf16[32,2,128,2,2,128]{5,2,4,3,1,0:T(8,128)(2,1)}), bf16[32,2,128,2,2,128]{5,2,4,3,1,0:T(8,128)(2,1)}, u32[]{:S(2)}, u32[]{:S(2)}) async-start(bf16[32,2,128,2,2,128]{5,2,4,3,1,0:T(8,128)(2,1)} %copy_select_fusion), calls=%async_computation.1 | async-start | bytes 16777216 | tf_op jit(solution)/shard_map/all_to_all | solution.py:80
  416.6 12.3 %collective-permute-start = (bf16[1,256,2,2,128]{4,1,2,0,3:T(8,128)(2,1)S(1)}, bf16[1,256,2,2,128]{4,1,2,0,3:T(8,128)(2,1)S(1)}, u32[]{:S(2)}, u32[]{:S(2)}) collective-permute-start(bf16[1,256,2,2,128]{4,1,2,0,3:T(8,128)(2,1)S(1)} %bitcast.87), channel_id=1, source_target_pairs={{0,8},{8,16},{16,24},{24,32},{32,40},{40,48},{48,56},{56,64},{64,7... | collective-permute-start | bytes 786440 | tf_op jit(solution)/shard_map/ppermute | solution.py:15
  428.8 6.1 %copy-start.1 = (bf16[2,128,4096]{2,1,0:T(8,128)(2,1)S(1)}, bf16[2,128,4096]{2,1,0:T(8,128)(2,1)}, u32[]{:S(2)}) copy-start(bf16[2,128,4096]{2,1,0:T(8,128)(2,1)} %param.10) | copy-start | bytes 6291460
Sparse Core Ops, SparseCore 0:
  44.6 108.6 all-reduce.1
Sparse Core Ops, SparseCore 1:
  47.5 83.2 all-gather.1
where the time goes:
time: 443 us; the launch traced here: 442 us
  waiting for transfers between devices  298 us (67%)
  local copies, waits for them, and re-layouts  54.6 us (12%)
  other arithmetic  23.7 us (5%)
  matrix products  21.9 us (5%)
  blocking collectives  16.9 us (4%)
  between operations  15.1 us (3%)
  starting transfers between devices  12 us (3%)
    all_to_all x1, waiting for transfers between devices, on_device(): lax.all_to_all(picked, 'seq', split_axis=0, concat_axis=0, tiled=True)  199 us
    psum x1, waiting for transfers between devices, on_device(): enc_sum = lax.psum(partial_terms, 'head')  90.3 us
    unnamed x21, local copies, waits for them, and re-layouts  18.3 us
    gather x1, local copies, waits for them, and re-layouts, on_device(): jnp.take(memory, lax.all_to_all(wanted, 'seq', split_axis=0, concat_axis=...  18.3 us
    all_to_all x1, blocking collectives, on_device(): lax.all_to_all(wanted, 'seq', split_axis=0, concat_axis=0, tiled=True)  16.9 us
    reduce_sum x2, other arithmetic, rms_scale(): mean_square = jnp.mean(values * values, axis=-1, keepdims=True)  12.1 us
    all_to_all x1, starting transfers between devices, on_device(): lax.all_to_all(picked, 'seq', split_axis=0, concat_axis=0, tiled=True)  10 us
  transfers between devices with their start and end apart: 4, of which 3 were waited for; matrix products, arithmetic and copies ran while one was open for 3% of the time, Pallas kernels for 0%

commit v1 on v0

--- a/solution.py
+++ b/solution.py
@@ -51,7 +51,8 @@
     attended = attended.reshape(row_total, heads_here * head_size)
     out_weight = enc_out.reshape(heads_here * head_size, model_width)
     partial_terms = jnp.dot(attended, out_weight, preferred_element_type=jnp.float32)
-    enc_sum = lax.psum(partial_terms, "head")
+    parts = lax.all_gather(partial_terms, "head", axis=0, tiled=False)
+    enc_sum = parts.sum(axis=0)
     normed = rms_scale(corpus_flat.astype(jnp.float32) + enc_sum, gain_out).astype(jnp.bfloat16)
     memory_cols = heads_here * 2 * head_size
     shard_piece = lax.all_gather(cca_kv, "seq", axis=0, tiled=True)

time: 443 us -> 695 us (1.57)
  waiting for transfers between devices: 298 us -> 522 us
  other arithmetic: 23.7 us -> 51.3 us
    all_gather x0 -> x1, waiting for transfers between devices: none -> 291 us  [on_device(): parts = lax.all_gather(partial_terms, 'head', axis=0, tiled=False)]
    psum x1 -> x0, waiting for transfers between devices: 90.3 us -> none  [on_device(): enc_sum = lax.psum(partial_terms, 'head')]
    all_gather x1, waiting for transfers between devices: 0.02 us -> 30.5 us  [on_device(): shard_piece = lax.all_gather(cca_kv, 'seq', axis=0, tiled=True)]
    reduce_sum x0 -> x1, other arithmetic: none -> 24.4 us  [on_device(): enc_sum = parts.sum(axis=0)]
    unnamed x21 -> x23, local copies, waits for them, and re-layouts: 18.3 us -> 19.8 us
  transfers between devices with their start and end apart: 4 -> 4, of which waited for: 3 -> 4; matrix products, arithmetic and copies ran while one was open for 3% -> 7% of each run, Pallas kernels for 0% -> 0%
where the time goes in v1:
time: 695 us; the launch traced here: 693 us
  waiting for transfers between devices  522 us (75%)
  local copies, waits for them, and re-layouts  56.1 us (8%)
  other arithmetic  51.3 us (7%)
  matrix products  20.7 us (3%)
  blocking collectives  16.9 us (2%)
  between operations  13.6 us (2%)
  starting transfers between devices  12 us (2%)
    all_gather x1, waiting for transfers between devices, on_device(): parts = lax.all_gather(partial_terms, 'head', axis=0, tiled=False)  291 us
    all_to_all x1, waiting for transfers between devices, on_device(): lax.all_to_all(picked, 'seq', split_axis=0, concat_axis=0, tiled=True)  192 us
    all_gather x1, waiting for transfers between devices, on_device(): shard_piece = lax.all_gather(cca_kv, 'seq', axis=0, tiled=True)  30.5 us
    reduce_sum x1, other arithmetic, on_device(): enc_sum = parts.sum(axis=0)  24.4 us
    unnamed x23, local copies, waits for them, and re-layouts  19.8 us
    gather x1, local copies, waits for them, and re-layouts, on_device(): jnp.take(memory, lax.all_to_all(wanted, 'seq', split_axis=0, concat_axis=...  18.3 us
    all_to_all x1, blocking collectives, on_device(): lax.all_to_all(wanted, 'seq', split_axis=0, concat_axis=0, tiled=True)  16.9 us
  transfers between devices with their start and end apart: 4, of which 4 were waited for; matrix products, arithmetic and copies ran while one was open for 7% of the time, Pallas kernels for 0%

profile of v1, /device:TPU:104, one launch (start us, length us, event | category | flops | bytes accessed | tf_op | source)
XLA Modules:
  0.0 692.8 jit_solution(4225485770290809380)
XLA Ops:
  6.5 0.7 all-gather.4.cloned.1.call-update
  7.3 16.2 %copy.108 = bf16[4096,2,3,128]{0,3,2,1:T(8,128)(2,1)} copy(bf16[4096,2,3,128]{3,1,2,0:T(2,128)(2,1)} %param.9) | data formatting | bytes 12582912 | tf_op args[1]
  23.5 3.3 fusion.2
  27.1 1.7 fusion.4
  28.8 1.1 copy-done.4
  29.9 3.5 convolution_convert_fusion
  33.4 1.2 copy.109
  34.5 1.7 reshape.300
  36.3 1.0 fusion.49
  38.4 1.2 fusion.18
  39.8 4.4 fusion.21
  44.3 0.7 copy-done.8
  45.5 16.9 %all_to_all.20 = s32[32,1,2]{2,1,0:T(1,128)S(1)} all-to-all(s32[32,1,2]{2,1,0:T(1,128)S(1)} %bitcast.92), channel_id=1, replica_groups=mesh['seq'=32,'head'=8] {'seq'}, dimensions={0} | all-to-all | bytes 512 | tf_op jit(solution)/shard_map/all_to_all | solution.py:79
  62.9 30.5 %all-gather.4.cloned.1.call-done = bf16[4096,2,2,128]{3,2,1,0:T(2,128)(2,1)} async-done(((bf16[128,2,2,128]{3,2,1,0:T(2,128)(2,1)}), bf16[4096,2,2,128]{3,2,1,0:T(2,128)(2,1)}) %all-gather.4.cloned.1.call-update) | async-done | bytes 4194320 | tf_op jit(solution)/shard_map/all_gather | solution.py:58
  93.3 7.2 %reshape.303 = bf16[4096,512]{1,0:T(8,128)(2,1)} reshape(bf16[4096,2,2,128]{3,2,1,0:T(2,128)(2,1)} %all-gather.4.cloned.1.call-done) | data formatting | bytes 8388608 | tf_op jit(solution)/shard_map/reshape | solution.py:61
  100.5 291.3 %all-gather.6.cloned.1.call-done = f32[4096,4096]{1,0:T(8,128)} async-done(((f32[512,4096]{1,0:T(8,128)}), f32[4096,4096]{1,0:T(8,128)}) %all-gather.6.cloned.1.call-update) | async-done | bytes 67108880 | tf_op jit(solution)/shard_map/all_gather | solution.py:54
  391.9 24.4 %reduce_sum.73 = f32[512,4096]{1,0:T(8,128)} reduce(f32[8,512,4096]{2,1,0:T(8,128)} %bitcast.9, f32[]{:T(128)} %constant.68.clone.1), dimensions={0}, to_apply=%region_5.6 | reduce | flops 14680064 | bytes 75497472 | tf_op jit(solution)/shard_map/reduce_sum | solution.py:55
  416.2 5.9 multiply_reduce_fusion
  422.1 1.1 copy-done.2
  423.2 6.0 multiply_convert_fusion
  429.2 5.8 convolution_convert_fusion.1
  435.1 18.3 %gather_fusion = bf16[64,128,2,2,128]{4,3,2,1,0:T(2,128)(2,1)} fusion(bf16[4,128,2,2,128]{4,3,2,1,0:T(2,128)(2,1)S(1)} %reshape.304, s32[1024]{0:T(1024)S(1)} %pad_clamp_fusion.1), kind=kCustom, calls=%fused_computation | custom fusion | bytes 16777472 | tf_op jit(solution)/shard_map/jit(_take)/gather | solution.py:78
  453.5 7.7 %copy_select_fusion = bf16[32,2,128,2,2,128]{5,2,4,3,1,0:T(8,128)(2,1)} fusion(bf16[32,2,128,2,2,128]{5,4,3,2,1,0:T(2,128)(2,1)} %bitcast.83, pred[32,2]{1,0:T(8,128)(4,1)S(1)} %copy.107), kind=kLoop, calls=%fused_computation.10 | loop fusion | flops 4194304 | bytes 16777280 | tf_op jit(solution)/shard_map/jit(_take)/select_n | solution.py:78
  461.2 10.0 %all-to-all-start.1 = ((bf16[32,2,128,2,2,128]{5,2,4,3,1,0:T(8,128)(2,1)}), bf16[32,2,128,2,2,128]{5,2,4,3,1,0:T(8,128)(2,1)}, u32[]{:S(2)}, u32[]{:S(2)}) async-start(bf16[32,2,128,2,2,128]{5,2,4,3,1,0:T(8,128)(2,1)} %copy_select_fusion), calls=%async_computation.1 | async-start | bytes 16777216 | tf_op jit(solution)/shard_map/all_to_all | solution.py:81
  472.0 191.8 %all-to-all-done.1 = bf16[32,2,128,2,2,128]{5,2,4,3,1,0:T(8,128)(2,1)} async-done(((bf16[32,2,128,2,2,128]{5,2,4,3,1,0:T(8,128)(2,1)}), bf16[32,2,128,2,2,128]{5,2,4,3,1,0:T(8,128)(2,1)}, u32[]{:S(2)}, u32[]{:S(2)}) %all-to-all-start.1) | async-done | bytes 8388640 | tf_op jit(solution)/shard_map/all_to_all | solution.py:81
  663.9 4.3 gather_fusion.1
  668.5 1.9 collective-permute-start
  670.4 1.6 copy_select_fusion.1
  672.0 7.9 %collective-permute-done = bf16[1,256,2,2,128]{4,1,2,0,3:T(8,128)(2,1)S(1)} collective-permute-done((bf16[1,256,2,2,128]{4,1,2,0,3:T(8,128)(2,1)S(1)}, bf16[1,256,2,2,128]{4,1,2,0,3:T(8,128)(2,1)S(1)}, u32[]{:S(2)}, u32[]{:S(2)}) %collective-permute-start) | collective-permute-done | bytes 262176 | tf_op jit(solution)/shard_map/ppermute | solution.py:15
  679.9 3.1 fusion.55
  682.9 2.0 fusion.15
  685.0 1.0 copy.126
  (58 shorter events, 3.8 us)
Async XLA Ops:
  6.5 33.3 %copy-start = (bf16[2,128,4096]{2,1,0:T(8,128)(2,1)S(1)}, bf16[2,128,4096]{2,1,0:T(8,128)(2,1)}, u32[]{:S(2)}) copy-start(bf16[2,128,4096]{2,1,0:T(8,128)(2,1)} %param.10) | copy-start | bytes 6291460
  6.5 86.8 %all-gather.4.cloned.1.call-start = ((), (), s32[]{:S(2)}) async-start(), calls=%async_computation.2 | async-start | bytes 4325376 | tf_op jit(solution)/shard_map/all_gather | solution.py:58
  7.3 384.6 %all-gather.6.cloned.1.call-start = ((), (), s32[]{:S(2)}) async-start(), calls=%async_computation.3 | async-start | bytes 75497472 | tf_op jit(solution)/shard_map/all_gather | solution.py:54
  7.3 19.6 %copy-start.6 = (f32[4096]{0:T(1024)S(1)}, f32[4096]{0:T(1024)}, u32[]{:S(2)}) copy-start(f32[4096]{0:T(1024)} %param.12) | copy-start | bytes 49156
  23.5 3.5 copy-start.3
  27.1 2.8 copy-start.4
  44.3 0.7 copy-start.8
  416.2 7.0 %copy-start.2 = (f32[512,4096]{1,0:T(8,128)S(1)}, f32[512,4096]{1,0:T(8,128)}, u32[]{:S(2)}) copy-start(f32[512,4096]{1,0:T(8,128)} %reduce_sum.73) | copy-start | bytes 25165828
  416.2 7.0 %copy-start.7 = (f32[4096]{0:T(1024)S(1)}, f32[4096]{0:T(1024)}, u32[]{:S(2)}) copy-start(f32[4096]{0:T(1024)} %param.13) | copy-start | bytes 49156
  461.2 10.3 %copy-start.5 = (bf16[512,2,128]{2,1,0:T(2,128)(2,1)S(1)}, bf16[512,2,128]{2,1,0:T(2,128)(2,1)}, u32[]{:S(2)}) copy-start(bf16[512,2,128]{2,1,0:T(2,128)(2,1)} %param.14) | copy-start | bytes 786436
  461.2 202.6 %all-to-all-start.1 = ((bf16[32,2,128,2,2,128]{5,2,4,3,1,0:T(8,128)(2,1)}), bf16[32,2,128,2,2,128]{5,2,4,3,1,0:T(8,128)(2,1)}, u32[]{:S(2)}, u32[]{:S(2)}) async-start(bf16[32,2,128,2,2,128]{5,2,4,3,1,0:T(8,128)(2,1)} %copy_select_fusion), calls=%async_computation.1 | async-start | bytes 16777216 | tf_op jit(solution)/shard_map/all_to_all | solution.py:81
  668.5 11.4 %collective-permute-start = (bf16[1,256,2,2,128]{4,1,2,0,3:T(8,128)(2,1)S(1)}, bf16[1,256,2,2,128]{4,1,2,0,3:T(8,128)(2,1)S(1)}, u32[]{:S(2)}, u32[]{:S(2)}) collective-permute-start(bf16[1,256,2,2,128]{4,1,2,0,3:T(8,128)(2,1)S(1)} %bitcast.91), channel_id=1, source_target_pairs={{0,8},{8,16},{16,24},{24,32},{32,40},{40,48},{48,56},{56,64},{64,7... | collective-permute-start | bytes 786440 | tf_op jit(solution)/shard_map/ppermute | solution.py:15
  679.9 6.1 copy-start.1
Sparse Core Ops, SparseCore 0:
  9.9 83.3 all-gather.3
  95.2 296.6 all-gather.5
